TPU v7x, 256 devices: a whole 4x4x8 slice. The times are simulated.
256 devices in a mesh: seq: 32 (over y, z), tp: 8 (over x, core).
Axes of the slice: x: 4, y: 4, z: 8, core: 2. Of those that a mesh axis runs over, the one named last changes fastest.
Arguments:
- values_in: bfloat16 [16384, 8192], P('seq', 'tp'), may hold values from -6 to 6
- gates_in: bfloat16 [16384, 8192], P('seq', 'tp'), may hold values from -6 to 6
- keys_in: bfloat16 [16384, 1024], P('seq', 'tp'), may hold values from -6 to 6
- queries_in: bfloat16 [16384, 1024], P('seq', 'tp'), may hold values from -6 to 6
- log_decay: float32 [128, 16384], P('tp', 'seq'), may hold values from -2 to 0, as said below
- conv_values: float32 [4, 8192], P(None, 'tp'), may hold values from -3 to 3
- bias_values: float32 [8192], P('tp'), may hold values from -3 to 3
- conv_keys: float32 [4, 1024], P(None, 'tp'), may hold values from -3 to 3
- bias_keys: float32 [1024], P('tp'), may hold values from -3 to 3
- conv_queries: float32 [4, 1024], P(None, 'tp'), may hold values from -3 to 3
- bias_queries: float32 [1024], P('tp'), may hold values from -3 to 3
- skip_scale: float32 [128], P('tp'), may hold values from 0.5 to 1.5
- norm_gain: float32 [8192], P('tp'), may hold values from 0.1 to 1.9
- out_weight: bfloat16 [8192, 4096], P('tp'), may hold values from -0.09375 to 0.09375
Outputs:
- mixer_out: bfloat16 [16384, 4096], P('seq', 'tp')
Inputs may be any that keep to these rules, and one draw needn't show every extreme that they name: `log_decay`: every entry is below zero.
All inputs are finite; a program needn't handle non-finite values.
Results may differ from a plain program's by a relative error of at most 0.015.
Values may be sent and summed in bfloat16 or wider, within the bound.
A program may use at most 64 MiB of HBM per device.

v0:
```python
from functools import partial
import jax
import jax.numpy as jnp
from jax import lax
from jax.sharding import PartitionSpec as P

N = 128
HIGH = lax.Precision.HIGHEST
norm_epsilon = 1e-05


def passed_along(block, axis, distance):
    devices = range(lax.axis_size(axis))
    route = [(i - distance, i) for i in devices if i - distance in devices]
    return lax.ppermute(block, axis, route)


def causal_filter(padded, kernel_weights, conv_bias, row_total):
    width = kernel_weights.shape[0]
    running = jnp.broadcast_to(conv_bias[None, :], (row_total, conv_bias.shape[0]))
    for offset in range(width):
        running = running + kernel_weights[offset][None, :] * padded[
            offset : offset + row_total
        ].astype(jnp.float32)
    return jax.nn.silu(running).astype(jnp.bfloat16)


def block_terms(carried, inputs, per_group):
    values, keys_block, queries, logs = inputs
    row_total = values.shape[0]
    groups = keys_block.shape[1]
    cumulative = jnp.cumsum(logs, axis=1)
    scores = jnp.einsum("tgn,sgn->gts", queries, keys_block, preferred_element_type=jnp.float32)
    positions = lax.broadcasted_iota(jnp.int32, (row_total, row_total), 0)
    sources = lax.broadcasted_iota(jnp.int32, (row_total, row_total), 1)
    log_gaps = jnp.where(
        (positions >= sources)[None], cumulative[:, :, None] - cumulative[:, None, :], -jnp.inf
    )
    mixing = (
        jnp.exp(log_gaps).reshape(groups, per_group, row_total, row_total) * scores[:, None]
    ).astype(jnp.bfloat16)
    local_part = jnp.einsum("ghts,sghp->tghp", mixing, values, preferred_element_type=jnp.float32)
    growth = jnp.exp(cumulative).T.reshape(row_total, groups, per_group, 1)
    from_state = (
        jnp.einsum("tgn,ghnp->tghp", queries.astype(jnp.float32), carried, precision=HIGH) * growth
    )
    remaining = jnp.exp(cumulative[:, -1:] - cumulative).T.reshape(row_total, groups, per_group, 1)
    weighted_keys = keys_block.astype(jnp.float32)[:, :, None, :] * remaining
    fresh_state = jnp.einsum(
        "tghn,tghp->ghnp", weighted_keys, values.astype(jnp.float32), precision=HIGH
    )
    carried = jnp.exp(cumulative[:, -1]).reshape(groups, per_group, 1, 1) * carried + fresh_state
    return (carried, local_part + from_state)


def shards(
    values_in,
    gates_in,
    keys_in,
    queries_in,
    log_decay,
    conv_values,
    bias_values,
    conv_keys,
    bias_keys,
    conv_queries,
    bias_queries,
    skip_scale,
    norm_gain,
    out_weight,
):
    row_total = values_in.shape[0]
    head_count = log_decay.shape[0]
    inner_width = values_in.shape[1]
    head_size = inner_width // head_count
    key_width = keys_in.shape[1]
    groups = key_width // N
    per_group = head_count // groups
    margin = conv_values.shape[0] - 1
    rim_send = jnp.concatenate(
        [
            values_in[row_total - margin :],
            keys_in[row_total - margin :],
            queries_in[row_total - margin :],
        ],
        axis=1,
    )
    rim_rows = passed_along(rim_send, "seq", 1)
    values = causal_filter(
        jnp.concatenate([rim_rows[:, :inner_width], values_in], axis=0),
        conv_values,
        bias_values,
        row_total,
    )
    keys_all = causal_filter(
        jnp.concatenate([rim_rows[:, inner_width : inner_width + key_width], keys_in], axis=0),
        conv_keys,
        bias_keys,
        row_total,
    )
    queries_all = causal_filter(
        jnp.concatenate([rim_rows[:, inner_width + key_width :], queries_in], axis=0),
        conv_queries,
        bias_queries,
        row_total,
    )
    block_rows = min(row_total, 512)
    block_count = row_total // block_rows
    value_blocks = values.reshape(block_count, block_rows, groups, per_group, head_size)
    key_blocks = keys_all.reshape(block_count, block_rows, groups, N)
    query_blocks = queries_all.reshape(block_count, block_rows, groups, N)
    log_blocks = log_decay.reshape(head_count, block_count, block_rows).transpose(1, 0, 2)
    initial = jnp.zeros((groups, per_group, N, head_size), jnp.float32)
    local_end, outputs = lax.scan(
        partial(block_terms, per_group=per_group),
        initial,
        (value_blocks, key_blocks, query_blocks, log_blocks),
    )
    cumulative = jnp.cumsum(log_decay, axis=1)
    device_log = cumulative[:, -1]
    flat_end = local_end.reshape(head_count, N * head_size)
    all_logs = lax.all_gather(device_log[None, :], "seq", axis=0, tiled=True)
    inclusive = jnp.cumsum(all_logs, axis=0)
    own_index = lax.axis_index("seq")
    before_mine = lax.dynamic_index_in_dim(inclusive - all_logs, own_index, 0, keepdims=False)
    pieces = lax.all_gather(flat_end[None].astype(jnp.bfloat16), "seq", axis=0, tiled=True).astype(
        jnp.float32
    )
    shard_ids = jnp.arange(pieces.shape[0], dtype=jnp.int32)
    through_shard = jnp.take(inclusive, shard_ids, axis=0)
    exponent = jnp.where(
        (shard_ids < own_index)[:, None], before_mine[None, :] - through_shard, -jnp.inf
    )
    incoming = jnp.zeros_like(flat_end) + jnp.einsum(
        "kh,khm->hm", jnp.exp(exponent), pieces, precision=HIGH
    )
    incoming = incoming.reshape(groups, per_group, N, head_size)
    growth = jnp.exp(cumulative).T.reshape(row_total, groups, per_group, 1)
    query_rows = queries_all.reshape(row_total, groups, N).astype(jnp.float32)
    from_before = jnp.einsum("tgn,ghnp->tghp", query_rows, incoming, precision=HIGH) * growth
    mixed = outputs.reshape(row_total, groups, per_group, head_size) + from_before
    mixed = mixed + skip_scale.reshape(groups, per_group)[None, :, :, None] * values.reshape(
        row_total, groups, per_group, head_size
    ).astype(jnp.float32)
    gated_rows = mixed.reshape(row_total, groups, per_group * head_size) * jax.nn.silu(
        gates_in.reshape(row_total, groups, per_group * head_size).astype(jnp.float32)
    )
    mean_square = jnp.mean(gated_rows * gated_rows, axis=-1, keepdims=True)
    normed = (
        (
            gated_rows
            * lax.rsqrt(mean_square + norm_epsilon)
            * norm_gain.reshape(groups, per_group * head_size)
        )
        .astype(jnp.bfloat16)
        .reshape(row_total, inner_width)
    )
    local_sum = jnp.dot(normed, out_weight, preferred_element_type=jnp.float32)
    summed = lax.psum(local_sum.astype(jnp.bfloat16), "tp").astype(jnp.float32)
    column_width = summed.shape[1] // lax.axis_size("tp")
    result = lax.dynamic_slice_in_dim(summed, lax.axis_index("tp") * column_width, column_width, 1)
    return result.astype(jnp.bfloat16)


def solution(mesh):
    placed = (
        P("seq", "tp"),
        P("seq", "tp"),
        P("seq", "tp"),
        P("seq", "tp"),
        P("tp", "seq"),
        P(None, "tp"),
        P("tp"),
        P(None, "tp"),
        P("tp"),
        P(None, "tp"),
        P("tp"),
        P("tp"),
        P("tp"),
        P("tp", None),
    )
    return jax.shard_map(
        shards, mesh=mesh, in_specs=placed, out_specs=P("seq", "tp"), check_vma=False
    )
```

profile of v0, /device:TPU:8, one launch (start us, length us, event | category | flops | bytes accessed | tf_op | source)
XLA Modules:
  0.0 248.3 jit_solution(196115072066289706)
XLA Ops:
  6.6 0.8 slice.96
  7.4 0.7 slice.97
  8.1 0.7 slice.98
  8.8 0.3 copy.48
  9.0 3.8 %collective-permute-start = (bf16[3,1280]{0,1:T(8,128)(2,1)S(1)}, bf16[3,1280]{0,1:T(8,128)(2,1)S(1)}, u32[]{:S(2)}, u32[]{:S(2)}) collective-permute-start(bf16[3,1280]{0,1:T(8,128)(2,1)S(1)} %copy.48), channel_id=1, source_target_pairs={{0,8},{8,16},{16,24},{24,32},{32,40},{40,48},{48,56},{56,64},{64,7... | collective-permute-start | bytes 23048 | tf_op jit(solution)/shard_map/ppermute | solution.py:15
  12.9 1.2 reduce-window.12
  14.5 0.9 fusion.41
  15.4 0.8 slice_bitcast_fusion.3
  16.3 1.5 copy.49
  17.8 6.5 %collective-permute-done = bf16[3,1280]{0,1:T(8,128)(2,1)S(1)} collective-permute-done((bf16[3,1280]{0,1:T(8,128)(2,1)S(1)}, bf16[3,1280]{0,1:T(8,128)(2,1)S(1)}, u32[]{:S(2)}, u32[]{:S(2)}) %collective-permute-start) | collective-permute-done | bytes 7712 | tf_op jit(solution)/shard_map/ppermute | solution.py:15
  24.7 2.7 %multiply_convert_fusion.3 = bf16[512,1024]{0,1:T(8,128)(2,1)S(1)} fusion(bf16[512,1024]{0,1:T(8,128)(2,1)S(1)} %copy.49, bf16[3,1024]{0,1:T(8,128)(2,1)S(1)} %slice.127, f32[1024]{0:T(1024)S(1)} %bitcast.91, f32[1024]{0:T(1024)S(1)} %bitcast.92, f32[1024]{0:T(1024)S(1)} %bitcast.90, f32[1024]{0:T(1024)S(1)} %bitcast.89, f32[1024]{0:T(1024)S(1)} %copy-done.7), kind=kLoop, calls=%fused_computation.25 | loop fusion | flops 13631488 | bytes 2123776 | tf_op jit(solution)/shard_map/convert_element_type | solution.py:25
  27.4 2.4 fusion.18
  29.9 0.3 copy.55
  30.1 1.2 convert_element_type.126
  31.4 0.6 dynamic-slice.1
  32.9 62.4 %all-reduce = f32[512]{0:T(512)S(1)} all-reduce(f32[512]{0:T(512)S(1)} %dynamic-update-slice), channel_id=2, replica_groups=mesh['seq'=32,'tp'=8] {'seq'}, use_global_device_ids=true, to_apply=%add | all-reduce | flops 512 | bytes 4096
  95.5 0.6 gather_fusion
  96.3 1.3 copy.57
  97.6 0.8 iota_compare_fusion
  98.7 0.3 fusion.42
  99.0 1.0 fusion.25
  100.0 5.8 %fusion.2 = f32[16,64,512]{2,1,0:T(8,128)} fusion(bf16[512,16,64]{0,2,1:T(8,128)(2,1)S(1)} %bitcast.86, f32[512,512]{1,0:T(8,128)S(1)} %fusion.42, f32[16,512]{1,0:T(8,128)S(1)} %copy_bitcast_fusion.1, pred[512,512]{1,0:T(8,128)(4,1)S(1)} %copy-done.4), kind=kOutput, calls=%fused_computation.4 | convolution fusion | flops 553648128 | bytes 4489216 | tf_op jit(solution)/shard_map/while/body/eval_jaxpr/ghts,sghp->tghp/dot_general | solution.py:42
  105.8 22.5 %all-gather.3.cloned.1.call-done = bf16[32,16,8192]{2,1,0:T(8,128)(2,1)} async-done(((bf16[1,16,8192]{2,1,0:T(8,128)(2,1)}), bf16[32,16,8192]{2,1,0:T(8,128)(2,1)}) %all-gather.3.cloned.1.call-update) | async-done | bytes 8388624 | tf_op jit(solution)/shard_map/all_gather | solution.py:126
  128.3 16.9 %fusion = f32[16,1,8192]{2,1,0:T(1,128)S(1)} fusion(f32[32,16,1]{0,2,1:T(1,128)S(1)} %copy.58, bf16[32,16,8192]{2,1,0:T(8,128)(2,1)} %all-gather.3.cloned.1.call-done), kind=kOutput, calls=%fused_computation.2 | convolution fusion | flops 50331648 | bytes 8914944 | tf_op jit(solution)/shard_map/kh,khm->hm/dot_general | solution.py:134
  145.2 1.1 copy.73
  146.3 2.5 reshape.210
  148.7 3.2 %fusion.31 = f32[16,64,512]{2,1,0:T(8,128)S(1)} fusion(f32[16,128,64]{2,1,0:T(8,128)} %reshape.210, bf16[512,128]{1,0:T(8,128)(2,1)S(1)} %multiply_convert_fusion.6), kind=kOutput, calls=%fused_computation.54 | convolution fusion | flops 805306368 | bytes 2752512 | tf_op jit(solution)/shard_map/tgn,ghnp->tghp/dot_general | solution.py:140
  152.0 1.0 fusion.10
  153.2 0.7 multiply_reduce_fusion
  153.9 9.7 %convolution_convert_fusion = bf16[512,4096]{1,0:T(8,128)(2,1)} fusion(bf16[1024,4096]{1,0:T(8,128)(2,1)} %param.27, f32[512,1024]{0,1:T(8,128)S(1)} %get-tuple-element.18, f32[1024]{0:T(1024)S(1)} %copy-done.12, f32[512]{0:T(512)S(1)} %add_rsqrt_fusion), kind=kOutput, calls=%fused_computation.6 | convolution fusion | flops 4298637312 | bytes 14686208 | tf_op jit(solution)/shard_map/dot_general | solution.py:158
  163.7 75.9 %all-reduce.3.cloned.1.call-done = bf16[512,4096]{1,0:T(8,128)(2,1)} async-done(((bf16[512,4096]{1,0:T(8,128)(2,1)}), bf16[512,4096]{1,0:T(8,128)(2,1)}) %all-reduce.3.cloned.1.call-update) | async-done | bytes 4194320 | tf_op jit(solution)/shard_map/psum | solution.py:159
  239.6 1.9 convert_convert_fusion
  (59 shorter events, 2.1 us)
Async XLA Ops:
  6.5 6.3 %copy-start = (f32[16,512]{1,0:T(8,128)S(1)}, f32[16,512]{1,0:T(8,128)}, u32[]{:S(2)}) copy-start(f32[16,512]{1,0:T(8,128)} %param.18) | copy-start | bytes 98308
  6.5 17.9 %copy-start.5 = (bf16[512,128]{1,0:T(8,128)(2,1)S(1)}, bf16[512,128]{1,0:T(8,128)(2,1)}, u32[]{:S(2)}) copy-start(bf16[512,128]{1,0:T(8,128)(2,1)} %param.16) | copy-start | bytes 393220
  6.5 17.9 %copy-start.9 = (f32[128]{0:T(128)S(1)}, f32[128]{0:T(128)}, u32[]{:S(2)}) copy-start(f32[128]{0:T(128)} %param.22) | copy-start | bytes 1540
  6.5 18.2 %copy-start.7 = (f32[1024]{0:T(1024)S(1)}, f32[1024]{0:T(1024)}, u32[]{:S(2)}) copy-start(f32[1024]{0:T(1024)} %param.20) | copy-start | bytes 12292
  6.5 121.8 %all-gather.3.cloned.1.call-start = ((), (), s32[]{:S(2)}) async-start(), calls=%async_computation | async-start | bytes 8650752 | tf_op jit(solution)/shard_map/all_gather | solution.py:126
  9.0 15.4 %collective-permute-start = (bf16[3,1280]{0,1:T(8,128)(2,1)S(1)}, bf16[3,1280]{0,1:T(8,128)(2,1)S(1)}, u32[]{:S(2)}, u32[]{:S(2)}) collective-permute-start(bf16[3,1280]{0,1:T(8,128)(2,1)S(1)} %copy.48), channel_id=1, source_target_pairs={{0,8},{8,16},{16,24},{24,32},{32,40},{40,48},{48,56},{56,64},{64,7... | collective-permute-start | bytes 23048 | tf_op jit(solution)/shard_map/ppermute | solution.py:15
  27.4 4.0 %copy-start.13 = (u32[256]{0:T(256)S(1)}, u32[256]{0:T(256)}, u32[]{:S(2)}) copy-start(u32[256]{0:T(256)} %constant.80) | copy-start | bytes 3076
  27.4 68.9 %copy-start.3 = (bf16[512,1024]{1,0:T(8,128)(2,1)S(1)}, bf16[512,1024]{1,0:T(8,128)(2,1)}, u32[]{:S(2)}) copy-start(bf16[512,1024]{1,0:T(8,128)(2,1)} %param.15) | copy-start | bytes 3145732
  29.8 68.6 %copy-start.8 = (f32[4,128]{1,0:T(4,128)S(1)}, f32[4,128]{1,0:T(4,128)}, u32[]{:S(2)}) copy-start(f32[4,128]{1,0:T(4,128)} %param.23) | copy-start | bytes 6148
  29.8 68.7 %copy-start.6 = (bf16[512,128]{1,0:T(8,128)(2,1)S(1)}, bf16[512,128]{1,0:T(8,128)(2,1)}, u32[]{:S(2)}) copy-start(bf16[512,128]{1,0:T(8,128)(2,1)} %param.17) | copy-start | bytes 393220
  29.8 68.7 %copy-start.10 = (f32[128]{0:T(128)S(1)}, f32[128]{0:T(128)}, u32[]{:S(2)}) copy-start(f32[128]{0:T(128)} %param.24) | copy-start | bytes 1540
  31.4 208.2 %all-reduce.3.cloned.1.call-start = ((), (), s32[]{:S(2)}) async-start(), calls=%async_computation.1 | async-start | bytes 8388608 | tf_op jit(solution)/shard_map/psum | solution.py:159
  98.5 1.5 copy-start.4
  146.3 5.7 %copy-start.11 = (f32[16]{0:T(128)S(1)}, f32[16]{0:T(128)}, u32[]{:S(2)}) copy-start(f32[16]{0:T(128)} %param.25) | copy-start | bytes 196
  148.7 3.2 %copy-start.2 = (f32[16,64,512]{2,1,0:T(8,128)S(1)}, f32[16,64,512]{2,1,0:T(8,128)}, u32[]{:S(2)}) copy-start(f32[16,64,512]{2,1,0:T(8,128)} %fusion.2) | copy-start | bytes 6291460
  152.0 1.2 copy-start.1
  153.2 0.7 copy-start.12
Sparse Core Ops, SparseCore 0:
  31.5 96.7 all-gather.2
  163.8 75.7 all-reduce.2
where the time goes:
time: 249 us; the launch traced here: 248 us
  waiting for transfers between devices  105 us (42%)
  blocking collectives  62.4 us (25%)
  matrix products  39.3 us (16%)
  local copies, waits for them, and re-layouts  14.4 us (6%)
  between operations  14.3 us (6%)
  other arithmetic  8.96 us (4%)
  starting transfers between devices  3.9 us (2%)
    psum x1, waiting for transfers between devices, shards(): summed = lax.psum(local_sum.astype(jnp.bfloat16), 'tp').astype(jnp.float32)  75.9 us
    unnamed x1, blocking collectives  62.4 us
    all_gather x1, waiting for transfers between devices, shards(): lax.all_gather(flat_end[None].astype(jnp.bfloat16), 'seq', axis=0, tiled=...  22.5 us
    dot_general x1, matrix products, shards(): jnp.einsum('kh,khm->hm', jnp.exp(exponent), pieces, precision=HIGH)  16.9 us
    dot_general x1, matrix products, shards(): local_sum = jnp.dot(normed, out_weight, preferred_element_type=jnp.float32)  9.74 us
    ppermute x1, waiting for transfers between devices, passed_along(): return lax.ppermute(block, axis, route)  6.53 us
    dot_general x1, matrix products, block_terms(): jnp.einsum('ghts,sghp->tghp', mixing, values, preferred_element_type=jnp....  5.8 us
  transfers between devices with their start and end apart: 3, of which 3 were waited for; matrix products, arithmetic and copies ran while one was open for 7% of the time, Pallas kernels for 0%

commit v1 on v0

--- a/solution.py
+++ b/solution.py
@@ -7,6 +7,12 @@
 N = 128
 HIGH = lax.Precision.HIGHEST
 norm_epsilon = 1e-05
+
+
+def gather_from_all(x, axis, dim):
+    size = lax.axis_size(axis)
+    repeats = [size if d == dim else 1 for d in range(x.ndim)]
+    return lax.all_to_all(jnp.tile(x, repeats), axis, split_axis=dim, concat_axis=dim, tiled=True)
 
 
 def passed_along(block, axis, distance):
@@ -123,9 +129,7 @@
     inclusive = jnp.cumsum(all_logs, axis=0)
     own_index = lax.axis_index("seq")
     before_mine = lax.dynamic_index_in_dim(inclusive - all_logs, own_index, 0, keepdims=False)
-    pieces = lax.all_gather(flat_end[None].astype(jnp.bfloat16), "seq", axis=0, tiled=True).astype(
-        jnp.float32
-    )
+    pieces = gather_from_all(flat_end[None].astype(jnp.bfloat16), "seq", 0).astype(jnp.float32)
     shard_ids = jnp.arange(pieces.shape[0], dtype=jnp.int32)
     through_shard = jnp.take(inclusive, shard_ids, axis=0)
     exponent = jnp.where(

time: 249 us -> 420 us (1.69)
  blocking collectives: 62.4 us -> 239 us
  waiting for transfers between devices: 105 us -> 87.4 us
  starting transfers between devices: 3.9 us -> 13 us
    unnamed x1, blocking collectives: 62.4 us -> 239 us
    all_gather x1 -> x0, waiting for transfers between devices: 22.5 us -> none  [shards(): lax.all_gather(flat_end[None].astype(jnp.bfloat16), 'seq', axis=0, tiled=...]
    all_to_all x0 -> x1, starting transfers between devices: none -> 9.09 us  [gather_from_all(): lax.all_to_all(jnp.tile(x, repeats), axis, split_axis=dim, concat_axis=di...]
    psum x1, waiting for transfers between devices: 75.9 us -> 80.9 us  [shards(): summed = lax.psum(local_sum.astype(jnp.bfloat16), 'tp').astype(jnp.float32)]
    another operation x4 -> x5, local copies, waits for them, and re-layouts: 2.61 us -> 6.84 us  [the longest x1 4.24 us: gather_from_all(): jnp.tile(x, repeats)]
  transfers between devices with their start and end apart: 3 -> 3, of which waited for: 3 -> 2; matrix products, arithmetic and copies ran while one was open for 7% -> 4% of each run, Pallas kernels for 0% -> 0%
where the time goes in v1:
time: 420 us; the launch traced here: 419 us
  blocking collectives  239 us (57%)
  waiting for transfers between devices  87.4 us (21%)
  matrix products  39.3 us (9%)
  local copies, waits for them, and re-layouts  17.9 us (4%)
  between operations  14.4 us (3%)
  starting transfers between devices  13 us (3%)
  other arithmetic  8.93 us (2%)
    unnamed x1, blocking collectives  239 us
    psum x1, waiting for transfers between devices, shards(): summed = lax.psum(local_sum.astype(jnp.bfloat16), 'tp').astype(jnp.float32)  80.9 us
    dot_general x1, matrix products, shards(): jnp.einsum('kh,khm->hm', jnp.exp(exponent), pieces, precision=HIGH)  16.9 us
    dot_general x1, matrix products, shards(): local_sum = jnp.dot(normed, out_weight, preferred_element_type=jnp.float32)  9.73 us
    all_to_all x1, starting transfers between devices, gather_from_all(): lax.all_to_all(jnp.tile(x, repeats), axis, split_axis=dim, concat_axis=di...  9.09 us
  transfers between devices with their start and end apart: 3, of which 2 were waited for; matrix products, arithmetic and copies ran while one was open for 4% of the time, Pallas kernels for 0%

profile of v1, /device:TPU:8, one launch (start us, length us, event | category | flops | bytes accessed | tf_op | source)
XLA Modules:
  0.0 419.5 jit_solution(12147121156892636644)
XLA Ops:
  6.5 0.8 slice.96
  7.3 0.7 slice.97
  8.0 0.7 slice.98
  8.9 3.8 collective-permute-start
  12.8 1.2 reduce-window.12
  14.4 0.9 fusion.41
  15.3 0.8 slice_bitcast_fusion.3
  16.3 1.5 copy.49
  17.8 6.5 %collective-permute-done = bf16[3,1280]{0,1:T(8,128)(2,1)S(1)} collective-permute-done((bf16[3,1280]{0,1:T(8,128)(2,1)S(1)}, bf16[3,1280]{0,1:T(8,128)(2,1)S(1)}, u32[]{:S(2)}, u32[]{:S(2)}) %collective-permute-start) | collective-permute-done | bytes 7712 | tf_op jit(solution)/shard_map/ppermute | solution.py:21
  24.6 2.7 multiply_convert_fusion.3
  27.3 2.4 fusion.18
  29.7 0.3 copy.55
  30.0 0.5 convert_element_type.124
  30.5 4.2 %tile.2 = bf16[32,16,8192]{2,1,0:T(8,128)(2,1)} broadcast(bf16[16,8192]{1,0:T(8,128)(2,1)S(1)} %convert_element_type.124), dimensions={1,2} | broadcast | bytes 8650752 | tf_op jit(solution)/shard_map/tile | solution.py:15
  34.7 9.1 %all-to-all-start = ((bf16[32,16,8192]{2,1,0:T(8,128)(2,1)}), bf16[32,16,8192]{2,1,0:T(8,128)(2,1)}, u32[]{:S(2)}, u32[]{:S(2)}) async-start(bf16[32,16,8192]{2,1,0:T(8,128)(2,1)} %tile.2), calls=%async_computation | async-start | bytes 16777216 | tf_op jit(solution)/shard_map/all_to_all | solution.py:15
  43.9 0.6 dynamic-slice.1
  45.4 238.6 %all-reduce = f32[512]{0:T(512)S(1)} all-reduce(f32[512]{0:T(512)S(1)} %dynamic-update-slice), channel_id=2, replica_groups=mesh['seq'=32,'tp'=8] {'seq'}, use_global_device_ids=true, to_apply=%add | all-reduce | flops 512 | bytes 4096
  284.2 0.6 gather_fusion
  285.0 1.3 copy.57
  286.3 0.8 iota_compare_fusion
  287.4 0.3 fusion.42
  287.7 1.0 fusion.25
  288.7 5.8 %fusion.2 = f32[16,64,512]{2,1,0:T(8,128)} fusion(bf16[512,16,64]{0,2,1:T(8,128)(2,1)S(1)} %bitcast.86, f32[512,512]{1,0:T(8,128)S(1)} %fusion.42, f32[16,512]{1,0:T(8,128)S(1)} %copy_bitcast_fusion.1, pred[512,512]{1,0:T(8,128)(4,1)S(1)} %copy-done.4), kind=kOutput, calls=%fused_computation.4 | convolution fusion | flops 553648128 | bytes 4489216 | tf_op jit(solution)/shard_map/while/body/eval_jaxpr/ghts,sghp->tghp/dot_general | solution.py:48
  294.5 16.9 %fusion = f32[16,1,8192]{2,1,0:T(1,128)S(1)} fusion(f32[32,16,1]{0,2,1:T(1,128)S(1)} %copy.58, bf16[32,16,8192]{2,1,0:T(8,128)(2,1)} %all-to-all-done), kind=kOutput, calls=%fused_computation.2 | convolution fusion | flops 50331648 | bytes 8914944 | tf_op jit(solution)/shard_map/kh,khm->hm/dot_general | solution.py:138
  311.4 1.1 copy.73
  312.5 2.4 reshape.208
  314.9 3.2 fusion.31
  318.2 1.0 fusion.10
  319.4 0.7 multiply_reduce_fusion
  320.1 9.7 %convolution_convert_fusion = bf16[512,4096]{1,0:T(8,128)(2,1)} fusion(bf16[1024,4096]{1,0:T(8,128)(2,1)} %param.27, f32[512,1024]{0,1:T(8,128)S(1)} %get-tuple-element.18, f32[1024]{0:T(1024)S(1)} %copy-done.12, f32[512]{0:T(512)S(1)} %add_rsqrt_fusion), kind=kOutput, calls=%fused_computation.6 | convolution fusion | flops 4298637312 | bytes 14686208 | tf_op jit(solution)/shard_map/dot_general | solution.py:162
  329.9 80.9 %all-reduce.3.cloned.1.call-done = bf16[512,4096]{1,0:T(8,128)(2,1)} async-done(((bf16[512,4096]{1,0:T(8,128)(2,1)}), bf16[512,4096]{1,0:T(8,128)(2,1)}) %all-reduce.3.cloned.1.call-update) | async-done | bytes 4194320 | tf_op jit(solution)/shard_map/psum | solution.py:163
  410.7 1.9 convert_convert_fusion
  (59 shorter events, 2.3 us)
Async XLA Ops:
  6.5 6.3 %copy-start = (f32[16,512]{1,0:T(8,128)S(1)}, f32[16,512]{1,0:T(8,128)}, u32[]{:S(2)}) copy-start(f32[16,512]{1,0:T(8,128)} %param.18) | copy-start | bytes 98308
  6.5 17.8 %copy-start.5 = (bf16[512,128]{1,0:T(8,128)(2,1)S(1)}, bf16[512,128]{1,0:T(8,128)(2,1)}, u32[]{:S(2)}) copy-start(bf16[512,128]{1,0:T(8,128)(2,1)} %param.16) | copy-start | bytes 393220
  6.5 17.9 %copy-start.9 = (f32[128]{0:T(128)S(1)}, f32[128]{0:T(128)}, u32[]{:S(2)}) copy-start(f32[128]{0:T(128)} %param.22) | copy-start | bytes 1540
  6.5 18.1 %copy-start.7 = (f32[1024]{0:T(1024)S(1)}, f32[1024]{0:T(1024)}, u32[]{:S(2)}) copy-start(f32[1024]{0:T(1024)} %param.20) | copy-start | bytes 12292
  8.9 15.4 %collective-permute-start = (bf16[3,1280]{0,1:T(8,128)(2,1)S(1)}, bf16[3,1280]{0,1:T(8,128)(2,1)S(1)}, u32[]{:S(2)}, u32[]{:S(2)}) collective-permute-start(bf16[3,1280]{0,1:T(8,128)(2,1)S(1)} %copy.48), channel_id=1, source_target_pairs={{0,8},{8,16},{16,24},{24,32},{32,40},{40,48},{48,56},{56,64},{64,7... | collective-permute-start | bytes 23048 | tf_op jit(solution)/shard_map/ppermute | solution.py:21
  34.7 9.2 %copy-start.13 = (u32[256]{0:T(256)S(1)}, u32[256]{0:T(256)}, u32[]{:S(2)}) copy-start(u32[256]{0:T(256)} %constant.80) | copy-start | bytes 3076
  34.7 250.2 %copy-start.3 = (bf16[512,1024]{1,0:T(8,128)(2,1)S(1)}, bf16[512,1024]{1,0:T(8,128)(2,1)}, u32[]{:S(2)}) copy-start(bf16[512,1024]{1,0:T(8,128)(2,1)} %param.15) | copy-start | bytes 3145732
  34.7 259.8 %all-to-all-start = ((bf16[32,16,8192]{2,1,0:T(8,128)(2,1)}), bf16[32,16,8192]{2,1,0:T(8,128)(2,1)}, u32[]{:S(2)}, u32[]{:S(2)}) async-start(bf16[32,16,8192]{2,1,0:T(8,128)(2,1)} %tile.2), calls=%async_computation | async-start | bytes 16777216 | tf_op jit(solution)/shard_map/all_to_all | solution.py:15
  43.8 243.3 %copy-start.8 = (f32[4,128]{1,0:T(4,128)S(1)}, f32[4,128]{1,0:T(4,128)}, u32[]{:S(2)}) copy-start(f32[4,128]{1,0:T(4,128)} %param.23) | copy-start | bytes 6148
  43.8 243.3 %copy-start.6 = (bf16[512,128]{1,0:T(8,128)(2,1)S(1)}, bf16[512,128]{1,0:T(8,128)(2,1)}, u32[]{:S(2)}) copy-start(bf16[512,128]{1,0:T(8,128)(2,1)} %param.17) | copy-start | bytes 393220
  43.8 243.3 %copy-start.10 = (f32[128]{0:T(128)S(1)}, f32[128]{0:T(128)}, u32[]{:S(2)}) copy-start(f32[128]{0:T(128)} %param.24) | copy-start | bytes 1540
  43.9 366.9 %all-reduce.3.cloned.1.call-start = ((), (), s32[]{:S(2)}) async-start(), calls=%async_computation.1 | async-start | bytes 8388608 | tf_op jit(solution)/shard_map/psum | solution.py:163
  287.2 1.5 copy-start.4
  312.5 5.7 %copy-start.11 = (f32[16]{0:T(128)S(1)}, f32[16]{0:T(128)}, u32[]{:S(2)}) copy-start(f32[16]{0:T(128)} %param.25) | copy-start | bytes 196
  314.9 3.2 copy-start.2
  318.2 1.2 copy-start.1
  319.4 0.7 copy-start.12
Sparse Core Ops, SparseCore 0:
  330.0 80.7 all-reduce.2
